TPU v7x, 256 devices: a whole 4x4x8 slice. The times are simulated.
256 devices in a mesh: col: 32 (over x, y, core), sub: 8 (over z).
Axes of the slice: x: 4, y: 4, z: 8, core: 2. Of those that a mesh axis runs over, the one named last changes fastest.
Arguments:
- vectors: bfloat16 [1048576, 128], P(('col', 'sub')), may hold values from -6 to 6
- near_blocks: bfloat16 [4096, 4, 256, 256], P(('col', 'sub')), may hold values from -0.1875 to 0.1875
- near_index: int32 [4096, 4], P(('col', 'sub')), may hold values from 0 to 4095, as said below
- leaf_basis: bfloat16 [4096, 32, 256], P(('col', 'sub')), may hold values from -0.375 to 0.375
- leaf_transfer: float32 [4096, 32, 32], P(('col', 'sub')), may hold values from -0.25 to 0.25
- leaf_coupling: float32 [4096, 8, 32, 32], P(('col', 'sub')), may hold values from -0.375 to 0.375
- leaf_far: int32 [4096, 8], P(('col', 'sub')), may hold values from 0 to 4095, as said below
- cluster_transfer: float32 [256, 32, 32], P(('col', 'sub')), may hold values from -0.375 to 0.375
- cluster_coupling: float32 [256, 4, 32, 32], P(('col', 'sub')), may hold values from -0.5 to 0.5
- cluster_partner: int32 [256, 4], P(('col', 'sub')), may hold values from 0 to 7
- top_coupling: float32 [32, 8, 32, 32], P('col'), may hold values from -0.375 to 0.375
- top_partner: int32 [32, 8], P('col'), may hold values from 0 to 31
Outputs:
- products: bfloat16 [1048576, 128], P(('col', 'sub'))
Inputs may be any that keep to these rules, and one draw needn't show every extreme that they name: `near_index`: slot 0 of leaf i is i itself; every entry lies within 16 leaves of i; slot 1 is exactly 16 leaves away from i. `leaf_far`: every entry lies within 16 leaves of its row leaf i; slots 0 and 1 are exactly 16 leaves away from i.
All inputs are finite; a program needn't handle non-finite values.
Results may differ from a plain program's by a relative error of at most 0.0034.
Values may be sent and summed in bfloat16 or wider, within the bound.
A program may use at most 64 MiB of HBM per device.

v0:
```python
import jax
import jax.numpy as jnp
from jax import lax
from jax.sharding import PartitionSpec as P

HIGHEST = lax.Precision.HIGHEST


def with_halo(block, sides, width):
    for axis, dim in sides:
        count = lax.axis_size(axis)
        forward = [(i, i + 1) for i in range(count - 1)]
        backward = [(target, source) for source, target in forward]
        low = lax.ppermute(
            lax.slice_in_dim(block, block.shape[dim] - width, None, axis=dim), axis, forward
        )
        high = lax.ppermute(lax.slice_in_dim(block, 0, width, axis=dim), axis, backward)
        block = jnp.concatenate([low, block, high], axis=dim)
    return block


def local(
    vectors,
    near_blocks,
    near_index,
    leaf_basis,
    leaf_transfer,
    leaf_coupling,
    leaf_far,
    cluster_transfer,
    cluster_coupling,
    cluster_partner,
    top_coupling,
    top_partner,
):
    leaves_here = leaf_basis.shape[0]
    leaf_rows = leaf_basis.shape[2]
    columns = vectors.shape[1]
    window_start = lax.axis_index(("col", "sub")) * leaves_here - leaves_here
    widened = with_halo(vectors, ((("col", "sub"), 0),), leaves_here * leaf_rows)
    window_vec = widened.reshape(3 * leaves_here, leaf_rows, columns)
    own_vec = vectors.reshape(leaves_here, leaf_rows, columns)
    leaf_coefs = jnp.einsum("lrp,lpc->lrc", leaf_basis, own_vec, preferred_element_type=jnp.float32)
    window_coefs = with_halo(leaf_coefs, ((("col", "sub"), 0),), leaves_here)
    cluster_coef = jnp.einsum("lrs,lrc->sc", leaf_transfer, leaf_coefs, precision=HIGHEST)
    sub_coefs = lax.all_gather(cluster_coef[None], "sub", axis=0, tiled=True)
    cluster_field = jnp.einsum(
        "krs,ksc->rc", cluster_coupling[0], sub_coefs[cluster_partner[0]], precision=HIGHEST
    )
    upward = jnp.dot(cluster_transfer[0].T, cluster_coef, precision=HIGHEST)
    top_coef = lax.psum(upward, "sub")
    col_coefs = lax.all_gather(top_coef[None], "col", axis=0, tiled=True)
    top_field = jnp.einsum(
        "krs,ksc->rc", top_coupling[0], col_coefs[top_partner[0]], precision=HIGHEST
    )
    cluster_field = cluster_field + jnp.dot(cluster_transfer[0], top_field, precision=HIGHEST)
    far_coefs = window_coefs[leaf_far - window_start]
    leaf_field = jnp.einsum("lkrs,lksc->lrc", leaf_coupling, far_coefs, precision=HIGHEST)
    leaf_field = leaf_field + jnp.einsum(
        "lrs,sc->lrc", leaf_transfer, cluster_field, precision=HIGHEST
    )
    rounded = leaf_field.astype(jnp.bfloat16)
    picked = window_vec[near_index - window_start]
    near_part = jnp.einsum(
        "lkij,lkjc->lic", near_blocks, picked, preferred_element_type=jnp.float32
    )
    far_part = jnp.einsum("lrp,lrc->lpc", leaf_basis, rounded, preferred_element_type=jnp.float32)
    return (near_part + far_part).astype(jnp.bfloat16).reshape(leaves_here * leaf_rows, columns)


def solution(mesh):
    in_specs = (
        P(("col", "sub"), None),
        P(("col", "sub"), None, None, None),
        P(("col", "sub"), None),
        P(("col", "sub"), None, None),
        P(("col", "sub"), None, None),
        P(("col", "sub"), None, None, None),
        P(("col", "sub"), None),
        P(("col", "sub"), None, None),
        P(("col", "sub"), None, None, None),
        P(("col", "sub"), None),
        P("col", None, None, None),
        P("col", None),
    )
    out_specs = P(("col", "sub"), None)
    return jax.shard_map(local, mesh=mesh, in_specs=in_specs, out_specs=out_specs, check_vma=False)
```

profile of v0, /device:TPU:1, one launch (start us, length us, event | category | flops | bytes accessed | tf_op | source)
XLA Modules:
  0.0 154.2 jit_solution(7868082268854348627)
XLA Ops:
  0.0 1.7 %fusion.12 = f32[16,32,128]{2,1,0:T(8,128)S(1)} fusion(bf16[16,32,256]{2,1,0:T(8,128)(2,1)} %param.15, bf16[16,256,128]{2,1,0:T(8,128)(2,1)} %bitcast.79), kind=kOutput, calls=%fused_computation.33 | convolution fusion | flops 33554432 | bytes 1572864 | tf_op jit(solution)/shard_map/lrp,lpc->lrc/dot_general | solution.py:43
  1.7 8.9 %collective-permute-start.3 = (f32[16,32,128]{2,1,0:T(8,128)S(1)}, f32[16,32,128]{2,1,0:T(8,128)S(1)}, u32[]{:S(2)}, u32[]{:S(2)}) collective-permute-start(f32[16,32,128]{2,1,0:T(8,128)S(1)} %fusion.12), channel_id=1, source_target_pairs={{1,0},{2,1},{3,2},{4,3},{5,4},{6,5},{7,6},{8,7},{9,8},{10,9},{11,1... | collective-permute-start | bytes 786440 | tf_op jit(solution)/shard_map/ppermute | solution.py:17
  10.6 1.9 %collective-permute-start.2 = (f32[16,32,128]{2,1,0:T(8,128)S(1)}, f32[16,32,128]{2,1,0:T(8,128)}, u32[]{:S(2)}, u32[]{:S(2)}) collective-permute-start(f32[16,32,128]{2,1,0:T(8,128)S(1)} %fusion.12), channel_id=1, source_target_pairs={{0,1},{1,2},{2,3},{3,4},{4,5},{5,6},{6,7},{7,8},{8,9},{9,10},{10,1... | collective-permute-start | bytes 786440 | tf_op jit(solution)/shard_map/ppermute | solution.py:14
  12.5 4.9 %collective-permute-start.1 = (bf16[4096,128]{1,0:T(8,128)(2,1)}, bf16[4096,128]{1,0:T(8,128)(2,1)}, u32[]{:S(2)}, u32[]{:S(2)}) collective-permute-start(bf16[4096,128]{1,0:T(8,128)(2,1)} %param.12), channel_id=1, source_target_pairs={{1,0},{2,1},{3,2},{4,3},{5,4},{6,5},{7,6},{8,7},{9,8},{10,9},{11,1... | collective-permute-start | bytes 3145736 | tf_op jit(solution)/shard_map/ppermute | solution.py:17
  17.4 1.9 %collective-permute-start = (bf16[4096,128]{1,0:T(8,128)(2,1)}, bf16[4096,128]{1,0:T(8,128)(2,1)}, u32[]{:S(2)}, u32[]{:S(2)}) collective-permute-start(bf16[4096,128]{1,0:T(8,128)(2,1)} %param.12), channel_id=1, source_target_pairs={{0,1},{1,2},{2,3},{3,4},{4,5},{5,6},{6,7},{7,8},{8,9},{9,10},{10,1... | collective-permute-start | bytes 3145736 | tf_op jit(solution)/shard_map/ppermute | solution.py:14
  19.3 0.7 fusion.10
  20.0 0.7 fusion.11
  20.7 1.3 compare_select_fusion.1
  21.9 0.7 compare_select_fusion
  22.6 0.6 pad_clamp_fusion
  23.3 0.6 reshape.78
  23.9 1.5 fusion.13
  25.4 0.9 convolution_bitcast_fusion.3
  26.4 35.0 %psum.7 = f32[1,32,128]{2,1,0:T(8,128)S(1)} all-reduce(f32[1,32,128]{2,1,0:T(8,128)S(1)} %convolution_bitcast_fusion.3), channel_id=1, replica_groups=mesh['col'=32,'sub'=8] {'sub'}, use_global_device_ids=true, to_apply=%region_0.0 | all-reduce | flops 4096 | bytes 32768 | tf_op jit(solution)/shard_map/psum | solution.py:51
  61.4 18.5 %all-gather = f32[256,128]{1,0:T(8,128)S(1)} all-gather(f32[32,128]{1,0:T(8,128)S(1)} %bitcast.81), channel_id=2, replica_groups=mesh['col'=32,'sub'=8] {'sub'}, dimensions={0}, use_global_device_ids=true | all-gather | bytes 147456 | tf_op jit(solution)/shard_map/all_gather | solution.py:46
  79.9 36.2 %all_gather.7 = f32[32,32,128]{2,1,0:T(8,128)S(1)} all-gather(f32[1,32,128]{2,1,0:T(8,128)S(1)} %psum.7), channel_id=1, replica_groups=mesh['col'=32,'sub'=8] {'col'}, dimensions={0}, use_global_device_ids=true | all-gather | bytes 540672 | tf_op jit(solution)/shard_map/all_gather | solution.py:52
  116.1 0.6 gather_fusion.2
  116.6 0.2 convolution_bitcast_fusion.4
  116.9 0.7 gather_fusion.3
  117.6 0.3 convolution_bitcast_fusion.2
  117.9 0.6 pad_clamp_fusion.2
  118.5 0.7 copy.22
  119.4 0.9 fusion.4
  120.3 1.0 pad_maximum_fusion.1
  121.3 2.1 %gather_fusion.1 = f32[128,32,128]{2,1,0:T(8,128)} fusion(f32[48,32,128]{2,1,0:T(8,128)S(1)} %pad_maximum_fusion.1, s32[1024]{0:T(1024)S(1)} %pad_clamp_fusion.2), kind=kCustom, calls=%fused_computation.1 | custom fusion | bytes 4194816 | tf_op jit(solution)/shard_map/gather | solution.py:57
  123.4 4.4 %convolution_bitcast_fusion.1 = f32[16,32,128]{2,1,0:T(8,128)S(1)} fusion(f32[16,8,32,128]{3,2,1,0:T(8,128)} %bitcast.78, f32[16,8,32,32]{3,2,1,0:T(8,128)S(1)} %copy-done), kind=kOutput, calls=%fused_computation.10 | convolution fusion | flops 201326592 | bytes 2883584 | tf_op jit(solution)/shard_map/lkrs,lksc->lrc/dot_general | solution.py:58
  127.9 0.4 fusion.3
  128.2 1.9 %fusion.14 = f32[16,128,256]{2,1,0:T(8,128)} fusion(bf16[16,32,128]{2,1,0:T(8,128)(2,1)S(1)} %fusion.3, bf16[16,32,256]{2,1,0:T(8,128)(2,1)S(1)} %copy-done.2), kind=kOutput, calls=%fused_computation.35 | convolution fusion | flops 33554432 | bytes 2490368 | tf_op jit(solution)/shard_map/lrp,lrc->lpc/dot_general | solution.py:67
  130.1 9.8 %pad_maximum_fusion = bf16[12288,128]{1,0:T(8,128)(2,1)} fusion(bf16[4096,128]{1,0:T(8,128)(2,1)} %collective-permute-done.1, bf16[4096,128]{1,0:T(8,128)(2,1)S(1)} %copy-done.1, bf16[4096,128]{1,0:T(8,128)(2,1)} %collective-permute-done), kind=kLoop, calls=%fused_computation.4 | loop fusion | flops 9437184 | bytes 6291456 | tf_op jit(solution)/shard_map/concatenate | solution.py:18
  139.9 4.9 %gather_fusion = bf16[64,256,128]{2,1,0:T(8,128)(2,1)} fusion(bf16[48,256,128]{2,1,0:T(8,128)(2,1)} %bitcast.76, s32[1024]{0:T(1024)S(1)} %pad_clamp_fusion.3), kind=kCustom, calls=%fused_computation | custom fusion | bytes 8388864 | tf_op jit(solution)/shard_map/gather | solution.py:63
  144.8 8.1 %fusion.1 = bf16[16,256,128]{1,2,0:T(8,128)(2,1)S(1)} fusion(f32[16,128,256]{2,1,0:T(8,128)} %fusion.14, bf16[16,4,256,128]{3,2,1,0:T(8,128)(2,1)} %bitcast.77, bf16[16,4,256,256]{3,2,1,0:T(8,128)(2,1)} %param.13), kind=kOutput, calls=%fused_computation.7 | convolution fusion | flops 1074790400 | bytes 15728640 | tf_op jit(solution)/shard_map/lkij,lkjc->lic/dot_general | solution.py:64
  152.9 1.3 copy.26
  (20 shorter events, 0.2 us)
Async XLA Ops:
  0.0 123.4 %copy-start = (f32[16,8,32,32]{3,2,1,0:T(8,128)S(1)}, f32[16,8,32,32]{3,2,1,0:T(8,128)}, u32[]{:S(2)}) copy-start(f32[16,8,32,32]{3,2,1,0:T(8,128)} %param.17) | copy-start | bytes 1572868
  0.0 116.6 %copy-start.5 = (f32[1,4,32,32]{3,2,1,0:T(8,128)S(1)}, f32[1,4,32,32]{3,2,1,0:T(8,128)}, u32[]{:S(2)}) copy-start(f32[1,4,32,32]{3,2,1,0:T(8,128)} %param.20) | copy-start | bytes 49156
  0.0 117.6 %copy-start.4 = (f32[1,8,32,32]{3,2,1,0:T(8,128)S(1)}, f32[1,8,32,32]{3,2,1,0:T(8,128)}, u32[]{:S(2)}) copy-start(f32[1,8,32,32]{3,2,1,0:T(8,128)} %param.22) | copy-start | bytes 98308
  1.7 118.5 %collective-permute-start.3 = (f32[16,32,128]{2,1,0:T(8,128)S(1)}, f32[16,32,128]{2,1,0:T(8,128)S(1)}, u32[]{:S(2)}, u32[]{:S(2)}) collective-permute-start(f32[16,32,128]{2,1,0:T(8,128)S(1)} %fusion.12), channel_id=1, source_target_pairs={{1,0},{2,1},{3,2},{4,3},{5,4},{6,5},{7,6},{8,7},{9,8},{10,9},{11,1... | collective-permute-start | bytes 786440 | tf_op jit(solution)/shard_map/ppermute | solution.py:17
  10.6 109.6 %collective-permute-start.2 = (f32[16,32,128]{2,1,0:T(8,128)S(1)}, f32[16,32,128]{2,1,0:T(8,128)}, u32[]{:S(2)}, u32[]{:S(2)}) collective-permute-start(f32[16,32,128]{2,1,0:T(8,128)S(1)} %fusion.12), channel_id=1, source_target_pairs={{0,1},{1,2},{2,3},{3,4},{4,5},{5,6},{6,7},{7,8},{8,9},{9,10},{10,1... | collective-permute-start | bytes 786440 | tf_op jit(solution)/shard_map/ppermute | solution.py:14
  12.5 117.6 %collective-permute-start.1 = (bf16[4096,128]{1,0:T(8,128)(2,1)}, bf16[4096,128]{1,0:T(8,128)(2,1)}, u32[]{:S(2)}, u32[]{:S(2)}) collective-permute-start(bf16[4096,128]{1,0:T(8,128)(2,1)} %param.12), channel_id=1, source_target_pairs={{1,0},{2,1},{3,2},{4,3},{5,4},{6,5},{7,6},{8,7},{9,8},{10,9},{11,1... | collective-permute-start | bytes 3145736 | tf_op jit(solution)/shard_map/ppermute | solution.py:17
  17.4 112.7 %collective-permute-start = (bf16[4096,128]{1,0:T(8,128)(2,1)}, bf16[4096,128]{1,0:T(8,128)(2,1)}, u32[]{:S(2)}, u32[]{:S(2)}) collective-permute-start(bf16[4096,128]{1,0:T(8,128)(2,1)} %param.12), channel_id=1, source_target_pairs={{0,1},{1,2},{2,3},{3,4},{4,5},{5,6},{6,7},{7,8},{8,9},{9,10},{10,1... | collective-permute-start | bytes 3145736 | tf_op jit(solution)/shard_map/ppermute | solution.py:14
  123.4 4.4 %copy-start.3 = (f32[16,32,32]{2,1,0:T(8,128)S(1)}, f32[16,32,32]{2,1,0:T(8,128)}, u32[]{:S(2)}) copy-start(f32[16,32,32]{2,1,0:T(8,128)} %param.16) | copy-start | bytes 196612
  123.4 4.8 %copy-start.2 = (bf16[16,32,256]{2,1,0:T(8,128)(2,1)S(1)}, bf16[16,32,256]{2,1,0:T(8,128)(2,1)}, u32[]{:S(2)}) copy-start(bf16[16,32,256]{2,1,0:T(8,128)(2,1)} %param.15) | copy-start | bytes 786436
  123.4 6.7 %copy-start.1 = (bf16[4096,128]{1,0:T(8,128)(2,1)S(1)}, bf16[4096,128]{1,0:T(8,128)(2,1)}, u32[]{:S(2)}) copy-start(bf16[4096,128]{1,0:T(8,128)(2,1)} %param.12) | copy-start | bytes 3145732
where the time goes:
time: 155 us; the launch traced here: 154 us
  blocking collectives  89.7 us (58%)
  matrix products  20.3 us (13%)
  starting transfers between devices  17.6 us (11%)
  other arithmetic  15.3 us (10%)
  local copies, waits for them, and re-layouts  11.1 us (7%)
    all_gather x1, blocking collectives, local(): col_coefs = lax.all_gather(top_coef[None], 'col', axis=0, tiled=True)  36.2 us
    psum x1, blocking collectives, local(): top_coef = lax.psum(upward, 'sub')  35 us
    all_gather x1, blocking collectives, local(): sub_coefs = lax.all_gather(cluster_coef[None], 'sub', axis=0, tiled=True)  18.5 us
    ppermute x2, starting transfers between devices, with_halo(): lax.ppermute(lax.slice_in_dim(block, 0, width, axis=dim), axis, backward)  13.7 us
    concatenate x2, other arithmetic, with_halo(): block = jnp.concatenate([low, block, high], axis=dim)  10.8 us
    dot_general x1, matrix products, local(): jnp.einsum('lkij,lkjc->lic', near_blocks, picked, preferred_element_type=...  8.06 us
    gather x1, local copies, waits for them, and re-layouts, local(): picked = window_vec[near_index - window_start]  4.91 us
    dot_general x1, matrix products, local(): jnp.einsum('lkrs,lksc->lrc', leaf_coupling, far_coefs, precision=HIGHEST)  4.43 us
  transfers between devices with their start and end apart: 4, of which 0 were waited for; matrix products, arithmetic and copies ran while one was open for 14% of the time, Pallas kernels for 0%

commit v1 on v0

--- a/solution.py
+++ b/solution.py
@@ -43,7 +43,9 @@
     leaf_coefs = jnp.einsum("lrp,lpc->lrc", leaf_basis, own_vec, preferred_element_type=jnp.float32)
     window_coefs = with_halo(leaf_coefs, ((("col", "sub"), 0),), leaves_here)
     cluster_coef = jnp.einsum("lrs,lrc->sc", leaf_transfer, leaf_coefs, precision=HIGHEST)
-    sub_coefs = lax.all_gather(cluster_coef[None], "sub", axis=0, tiled=True)
+    sub_coefs = jnp.concatenate(
+        lax.all_to_all(jnp.stack([cluster_coef[None]] * lax.axis_size("sub")), "sub", 0, 0), axis=0
+    )
     cluster_field = jnp.einsum(
         "krs,ksc->rc", cluster_coupling[0], sub_coefs[cluster_partner[0]], precision=HIGHEST
     )

time: 155 us -> 132 us (0.85)
  blocking collectives: 89.7 us -> 63.3 us
  starting transfers between devices: 17.6 us -> 23 us
  other arithmetic: 15.3 us -> 13.5 us
    all_gather x1 -> x0, blocking collectives: 18.5 us -> none  [local(): sub_coefs = lax.all_gather(cluster_coef[None], 'sub', axis=0, tiled=True)]
    all_gather x1, blocking collectives: 36.2 us -> 30.1 us  [local(): col_coefs = lax.all_gather(top_coef[None], 'col', axis=0, tiled=True)]
    all_to_all x0 -> x1, starting transfers between devices: none -> 5.46 us  [local(): lax.all_to_all(jnp.stack([cluster_coef[None]] * lax.axis_size('sub')), 's...]
    psum x1, blocking collectives: 35 us -> 33.2 us  [local(): top_coef = lax.psum(upward, 'sub')]
  transfers between devices with their start and end apart: 4 -> 5, of which waited for: 0 -> 0; matrix products, arithmetic and copies ran while one was open for 14% -> 15% of each run, Pallas kernels for 0% -> 0%
where the time goes in v1:
time: 132 us
  blocking collectives  63.3 us (48%)
  starting transfers between devices  23 us (17%)
  matrix products  21.2 us (16%)
  other arithmetic  13.5 us (10%)
  local copies, waits for them, and re-layouts  10.5 us (8%)
    psum x1, blocking collectives, local(): top_coef = lax.psum(upward, 'sub')  33.2 us
    all_gather x1, blocking collectives, local(): col_coefs = lax.all_gather(top_coef[None], 'col', axis=0, tiled=True)  30.1 us
    ppermute x2, starting transfers between devices, with_halo(): lax.ppermute(lax.slice_in_dim(block, 0, width, axis=dim), axis, backward)  13.7 us
    concatenate x2, other arithmetic, with_halo(): block = jnp.concatenate([low, block, high], axis=dim)  10.8 us
    dot_general x1, matrix products, local(): jnp.einsum('lkij,lkjc->lic', near_blocks, picked, preferred_element_type=...  8.07 us
    all_to_all x1, starting transfers between devices, local(): lax.all_to_all(jnp.stack([cluster_coef[None]] * lax.axis_size('sub')), 's...  5.46 us
    gather x1, local copies, waits for them, and re-layouts, local(): picked = window_vec[near_index - window_start]  4.91 us
    dot_general x1, matrix products, local(): jnp.einsum('lkrs,lksc->lrc', leaf_coupling, far_coefs, precision=HIGHEST)  4.43 us
  transfers between devices with their start and end apart: 5, of which 0 were waited for; matrix products, arithmetic and copies ran while one was open for 15% of the time, Pallas kernels for 0%

profile of v1, /device:TPU:1, one launch (start us, length us, event | category | flops | bytes accessed | tf_op | source)
XLA Modules:
  0.0 131.6 jit_solution(12802998101694507040)
XLA Ops:
  0.0 1.7 %fusion.12 = f32[16,32,128]{2,1,0:T(8,128)S(1)} fusion(bf16[16,32,256]{2,1,0:T(8,128)(2,1)} %param.15, bf16[16,256,128]{2,1,0:T(8,128)(2,1)} %bitcast.79), kind=kOutput, calls=%fused_computation.33 | convolution fusion | flops 33554432 | bytes 1572864 | tf_op jit(solution)/shard_map/lrp,lpc->lrc/dot_general | solution.py:43
  1.7 8.9 %collective-permute-start.3 = (f32[16,32,128]{2,1,0:T(8,128)S(1)}, f32[16,32,128]{2,1,0:T(8,128)S(1)}, u32[]{:S(2)}, u32[]{:S(2)}) collective-permute-start(f32[16,32,128]{2,1,0:T(8,128)S(1)} %fusion.12), channel_id=1, source_target_pairs={{1,0},{2,1},{3,2},{4,3},{5,4},{6,5},{7,6},{8,7},{9,8},{10,9},{11,1... | collective-permute-start | bytes 786440 | tf_op jit(solution)/shard_map/ppermute | solution.py:17
  10.6 1.9 %collective-permute-start.2 = (f32[16,32,128]{2,1,0:T(8,128)S(1)}, f32[16,32,128]{2,1,0:T(8,128)}, u32[]{:S(2)}, u32[]{:S(2)}) collective-permute-start(f32[16,32,128]{2,1,0:T(8,128)S(1)} %fusion.12), channel_id=1, source_target_pairs={{0,1},{1,2},{2,3},{3,4},{4,5},{5,6},{6,7},{7,8},{8,9},{9,10},{10,1... | collective-permute-start | bytes 786440 | tf_op jit(solution)/shard_map/ppermute | solution.py:14
  12.5 4.9 %collective-permute-start.1 = (bf16[4096,128]{1,0:T(8,128)(2,1)}, bf16[4096,128]{1,0:T(8,128)(2,1)}, u32[]{:S(2)}, u32[]{:S(2)}) collective-permute-start(bf16[4096,128]{1,0:T(8,128)(2,1)} %param.12), channel_id=1, source_target_pairs={{1,0},{2,1},{3,2},{4,3},{5,4},{6,5},{7,6},{8,7},{9,8},{10,9},{11,1... | collective-permute-start | bytes 3145736 | tf_op jit(solution)/shard_map/ppermute | solution.py:17
  17.4 1.9 %collective-permute-start = (bf16[4096,128]{1,0:T(8,128)(2,1)}, bf16[4096,128]{1,0:T(8,128)(2,1)}, u32[]{:S(2)}, u32[]{:S(2)}) collective-permute-start(bf16[4096,128]{1,0:T(8,128)(2,1)} %param.12), channel_id=1, source_target_pairs={{0,1},{1,2},{2,3},{3,4},{4,5},{5,6},{6,7},{7,8},{8,9},{9,10},{10,1... | collective-permute-start | bytes 3145736 | tf_op jit(solution)/shard_map/ppermute | solution.py:14
  19.3 1.5 %fusion.13 = f32[128,32,1]{0,1,2:T(8,128)S(1)} fusion(f32[16,32,128]{2,1,0:T(8,128)S(1)} %fusion.12, f32[16,32,32]{2,1,0:T(8,128)} %param.16), kind=kOutput, calls=%fused_computation.34 | convolution fusion | flops 25165824 | bytes 344064 | tf_op jit(solution)/shard_map/lrs,lrc->sc/dot_general | solution.py:45
  20.9 0.7 stack.3
  21.5 5.5 %all-to-all-start = ((f32[8,1,32,128]{3,2,1,0:T(8,128)}), f32[8,1,32,128]{3,2,1,0:T(8,128)S(1)}, u32[]{:S(2)}, u32[]{:S(2)}) async-start(f32[8,1,32,128]{3,2,1,0:T(8,128)} %stack.3), calls=%async_computation | async-start | bytes 262144 | tf_op jit(solution)/shard_map/all_to_all | solution.py:47
  27.0 0.7 fusion.10
  27.6 0.7 fusion.11
  28.3 0.7 compare_select_fusion.1
  29.0 0.7 compare_select_fusion
  29.8 0.1 reshape.84
  29.9 0.1 copy.22
  30.0 0.1 reshape.76
  30.0 0.9 convolution_bitcast_fusion.3
  31.0 33.2 %psum.7 = f32[1,32,128]{2,1,0:T(8,128)S(1)} all-reduce(f32[1,32,128]{2,1,0:T(8,128)S(1)} %convolution_bitcast_fusion.3), channel_id=1, replica_groups=mesh['col'=32,'sub'=8] {'sub'}, use_global_device_ids=true, to_apply=%region_0.0 | all-reduce | flops 4096 | bytes 32768 | tf_op jit(solution)/shard_map/psum | solution.py:53
  64.2 30.1 %all_gather.3 = f32[32,32,128]{2,1,0:T(8,128)S(1)} all-gather(f32[1,32,128]{2,1,0:T(8,128)S(1)} %psum.7), channel_id=1, replica_groups=mesh['col'=32,'sub'=8] {'col'}, dimensions={0}, use_global_device_ids=true | all-gather | bytes 540672 | tf_op jit(solution)/shard_map/all_gather | solution.py:54
  94.2 0.6 gather_fusion.3
  94.8 0.3 convolution_bitcast_fusion.2
  95.2 0.6 gather_fusion.2
  95.7 1.1 convolution_bitcast_fusion.4
  96.8 0.9 fusion.4
  97.7 1.0 pad_maximum_fusion.1
  98.7 2.1 %gather_fusion.1 = f32[128,32,128]{2,1,0:T(8,128)} fusion(f32[48,32,128]{2,1,0:T(8,128)S(1)} %pad_maximum_fusion.1, s32[1024]{0:T(1024)S(1)} %pad_clamp_fusion.2), kind=kCustom, calls=%fused_computation.1 | custom fusion | bytes 4194816 | tf_op jit(solution)/shard_map/gather | solution.py:59
  100.9 4.4 %convolution_bitcast_fusion.1 = f32[16,32,128]{2,1,0:T(8,128)S(1)} fusion(f32[16,8,32,128]{3,2,1,0:T(8,128)} %bitcast.78, f32[16,8,32,32]{3,2,1,0:T(8,128)S(1)} %copy-done), kind=kOutput, calls=%fused_computation.10 | convolution fusion | flops 201326592 | bytes 2883584 | tf_op jit(solution)/shard_map/lkrs,lksc->lrc/dot_general | solution.py:60
  105.3 0.4 fusion.3
  105.7 1.9 %fusion.14 = f32[16,128,256]{2,1,0:T(8,128)} fusion(bf16[16,32,128]{2,1,0:T(8,128)(2,1)S(1)} %fusion.3, bf16[16,32,256]{2,1,0:T(8,128)(2,1)S(1)} %copy-done.2), kind=kOutput, calls=%fused_computation.35 | convolution fusion | flops 33554432 | bytes 2490368 | tf_op jit(solution)/shard_map/lrp,lrc->lpc/dot_general | solution.py:69
  107.6 9.8 %pad_maximum_fusion = bf16[12288,128]{1,0:T(8,128)(2,1)} fusion(bf16[4096,128]{1,0:T(8,128)(2,1)} %collective-permute-done.1, bf16[4096,128]{1,0:T(8,128)(2,1)S(1)} %copy-done.1, bf16[4096,128]{1,0:T(8,128)(2,1)} %collective-permute-done), kind=kLoop, calls=%fused_computation.4 | loop fusion | flops 9437184 | bytes 6291456 | tf_op jit(solution)/shard_map/concatenate | solution.py:18
  117.4 4.9 %gather_fusion = bf16[64,256,128]{2,1,0:T(8,128)(2,1)} fusion(bf16[48,256,128]{2,1,0:T(8,128)(2,1)} %bitcast.76, s32[1024]{0:T(1024)S(1)} %pad_clamp_fusion.3), kind=kCustom, calls=%fused_computation | custom fusion | bytes 8388864 | tf_op jit(solution)/shard_map/gather | solution.py:65
  122.3 8.1 %fusion.1 = bf16[16,256,128]{1,2,0:T(8,128)(2,1)S(1)} fusion(f32[16,128,256]{2,1,0:T(8,128)} %fusion.14, bf16[16,4,256,128]{3,2,1,0:T(8,128)(2,1)} %bitcast.77, bf16[16,4,256,256]{3,2,1,0:T(8,128)(2,1)} %param.13), kind=kOutput, calls=%fused_computation.7 | convolution fusion | flops 1074790400 | bytes 15728640 | tf_op jit(solution)/shard_map/lkij,lkjc->lic/dot_general | solution.py:66
  130.3 1.3 copy.26
  (20 shorter events, 0.1 us)
Async XLA Ops:
  0.0 100.9 %copy-start = (f32[16,8,32,32]{3,2,1,0:T(8,128)S(1)}, f32[16,8,32,32]{3,2,1,0:T(8,128)}, u32[]{:S(2)}) copy-start(f32[16,8,32,32]{3,2,1,0:T(8,128)} %param.17) | copy-start | bytes 1572868
  0.0 94.8 %copy-start.4 = (f32[1,8,32,32]{3,2,1,0:T(8,128)S(1)}, f32[1,8,32,32]{3,2,1,0:T(8,128)}, u32[]{:S(2)}) copy-start(f32[1,8,32,32]{3,2,1,0:T(8,128)} %param.22) | copy-start | bytes 98308
  1.7 96.0 %collective-permute-start.3 = (f32[16,32,128]{2,1,0:T(8,128)S(1)}, f32[16,32,128]{2,1,0:T(8,128)S(1)}, u32[]{:S(2)}, u32[]{:S(2)}) collective-permute-start(f32[16,32,128]{2,1,0:T(8,128)S(1)} %fusion.12), channel_id=1, source_target_pairs={{1,0},{2,1},{3,2},{4,3},{5,4},{6,5},{7,6},{8,7},{9,8},{10,9},{11,1... | collective-permute-start | bytes 786440 | tf_op jit(solution)/shard_map/ppermute | solution.py:17
  10.6 87.1 %collective-permute-start.2 = (f32[16,32,128]{2,1,0:T(8,128)S(1)}, f32[16,32,128]{2,1,0:T(8,128)}, u32[]{:S(2)}, u32[]{:S(2)}) collective-permute-start(f32[16,32,128]{2,1,0:T(8,128)S(1)} %fusion.12), channel_id=1, source_target_pairs={{0,1},{1,2},{2,3},{3,4},{4,5},{5,6},{6,7},{7,8},{8,9},{9,10},{10,1... | collective-permute-start | bytes 786440 | tf_op jit(solution)/shard_map/ppermute | solution.py:14
  12.5 95.0 %collective-permute-start.1 = (bf16[4096,128]{1,0:T(8,128)(2,1)}, bf16[4096,128]{1,0:T(8,128)(2,1)}, u32[]{:S(2)}, u32[]{:S(2)}) collective-permute-start(bf16[4096,128]{1,0:T(8,128)(2,1)} %param.12), channel_id=1, source_target_pairs={{1,0},{2,1},{3,2},{4,3},{5,4},{6,5},{7,6},{8,7},{9,8},{10,9},{11,1... | collective-permute-start | bytes 3145736 | tf_op jit(solution)/shard_map/ppermute | solution.py:17
  17.4 90.2 %collective-permute-start = (bf16[4096,128]{1,0:T(8,128)(2,1)}, bf16[4096,128]{1,0:T(8,128)(2,1)}, u32[]{:S(2)}, u32[]{:S(2)}) collective-permute-start(bf16[4096,128]{1,0:T(8,128)(2,1)} %param.12), channel_id=1, source_target_pairs={{0,1},{1,2},{2,3},{3,4},{4,5},{5,6},{6,7},{7,8},{8,9},{9,10},{10,1... | collective-permute-start | bytes 3145736 | tf_op jit(solution)/shard_map/ppermute | solution.py:14
  21.5 73.6 %all-to-all-start = ((f32[8,1,32,128]{3,2,1,0:T(8,128)}), f32[8,1,32,128]{3,2,1,0:T(8,128)S(1)}, u32[]{:S(2)}, u32[]{:S(2)}) async-start(f32[8,1,32,128]{3,2,1,0:T(8,128)} %stack.3), calls=%async_computation | async-start | bytes 262144 | tf_op jit(solution)/shard_map/all_to_all | solution.py:47
  100.9 4.4 %copy-start.3 = (f32[16,32,32]{2,1,0:T(8,128)S(1)}, f32[16,32,32]{2,1,0:T(8,128)}, u32[]{:S(2)}) copy-start(f32[16,32,32]{2,1,0:T(8,128)} %param.16) | copy-start | bytes 196612
  100.9 4.8 %copy-start.2 = (bf16[16,32,256]{2,1,0:T(8,128)(2,1)S(1)}, bf16[16,32,256]{2,1,0:T(8,128)(2,1)}, u32[]{:S(2)}) copy-start(bf16[16,32,256]{2,1,0:T(8,128)(2,1)} %param.15) | copy-start | bytes 786436
  100.9 6.7 %copy-start.1 = (bf16[4096,128]{1,0:T(8,128)(2,1)S(1)}, bf16[4096,128]{1,0:T(8,128)(2,1)}, u32[]{:S(2)}) copy-start(bf16[4096,128]{1,0:T(8,128)(2,1)} %param.12) | copy-start | bytes 3145732
